TPU v7x, 32 devices: a whole 2x2x4 slice. The times are simulated.
32 devices in a mesh: dp: 16 (over z, x, core), ctx: 2 (over y).
Axes of the slice: x: 2, y: 2, z: 4, core: 2. Of those that a mesh axis runs over, the one named last changes fastest.
Arguments:
- queries: bfloat16 [16, 512, 2048], P('dp', 'ctx'), may hold values from -48 to 48
- key_store: bfloat16 [16, 512, 2048], P('dp', 'ctx'), may hold values from -4 to 4
- value_store: bfloat16 [16, 512, 2048], P('dp', 'ctx'), may hold values from -5 to 5
- kv_exponents: int32 [16, 4, 16], P('dp', 'ctx'), may hold values from -1 to 1
- valid_length: int32 [16], P('dp'), may hold values from 64 to 512, as said below
- round_index: int32 [1], replicated, may hold values from 0 to 63
- out_grad: bfloat16 [16, 512, 2048], P('dp', None, 'ctx'), may hold values from -6 to 6
- params: bfloat16 [16, 2048, 2048], P('dp', None, 'ctx'), may hold values from -6 to 6
- tracker: bfloat16 [16, 2048, 2048], P('dp', None, 'ctx'), may hold values from -6 to 6
- old_grad: bfloat16 [16, 2048, 2048], P('dp', None, 'ctx'), may hold values from -6 to 6
Outputs:
- new_params: bfloat16 [16, 2048, 2048], P('dp', None, 'ctx')
- new_tracker: bfloat16 [16, 2048, 2048], P('dp', None, 'ctx')
Inputs may be any that keep to these rules, and one draw needn't show every extreme that they name: `valid_length`: every draw has a replica whose clip fills all 512 positions.
All inputs are finite; a program needn't handle non-finite values.
Results may differ from a plain program's by a relative error of at most 0.0053.
Values may be sent and summed in bfloat16 or wider, within the bound.
A program may use at most 128 MiB of HBM per device.

v0:
```python
import functools

import jax
import jax.numpy as jnp
from jax import lax
from jax.experimental import pallas as pl
from jax.experimental.pallas import tpu as pltpu
from jax.sharding import PartitionSpec as P


HEADS = 16
HD = 128
KBLK = 128
QROWS = 256
LAST_ROWS = 256
VMEM_LIMIT = 40 * 2**20
FLUSH_LIMIT = 16 * 2**20


step_size = 0.1
masked_score = -1e30


def from_partner(value, axis, bit):
    mask = 2**bit
    pairs = [(source, source ^ mask) for source in range(lax.axis_size(axis))]
    return lax.ppermute(value, axis, pairs)


def contract_rows(left_rows, right_rows):
    return lax.dot_general(
        left_rows, right_rows, (((0,), (0,)), ((), ())), preferred_element_type=jnp.float32
    )


def from_other(block):
    return lax.ppermute(block, "ctx", [(0, 1), (1, 0)])


def in_order(own, other, axis):
    first = lax.axis_index("ctx") == 0
    return jnp.concatenate(
        (jnp.where(first, own, other), jnp.where(first, other, own)), axis=axis
    )


def gather_ctx(block, axis):
    if lax.axis_size("ctx") != 2:
        return lax.all_gather(block, "ctx", axis=axis, tiled=True)
    return in_order(block, from_other(block), axis)


def rows_to_heads(block, group, groups):
    if lax.axis_size("ctx") != 2:
        return lax.all_to_all(block, "ctx", split_axis=1, concat_axis=0, tiled=True)
    width = block.shape[1] // (2 * groups)
    mine = lax.axis_index("ctx")
    kept = lax.dynamic_slice_in_dim(block, (mine * groups + group) * width, width, 1)
    sent = lax.dynamic_slice_in_dim(block, ((1 - mine) * groups + group) * width, width, 1)
    return in_order(kept, from_other(sent), 0)


def attend_kernel(step_heads, meta, scales, q_ref, k_ref, v_ref, out_ref):
    length = meta[0]
    seq = k_ref.shape[0]
    for local in range(step_heads):
        head = meta[1] + pl.program_id(0) * step_heads + local
        cols = pl.ds(local * HD, HD)

        def scaled(ref):
            return jnp.concatenate(
                [
                    (
                        ref[pl.ds(block * KBLK, KBLK), cols].astype(jnp.float32)
                        * scales[block, head]
                    ).astype(jnp.bfloat16)
                    for block in range(seq // KBLK)
                ],
                axis=0,
            )

        keys, values = scaled(k_ref), scaled(v_ref)
        for row0 in range(0, seq, QROWS):
            reach = row0 + QROWS
            scores = lax.dot_general(
                q_ref[pl.ds(row0, QROWS), cols],
                keys[:reach],
                (((1,), (1,)), ((), ())),
                preferred_element_type=jnp.float32,
            ) * (HD ** (-0.5))
            query_pos = row0 + lax.broadcasted_iota(jnp.int32, scores.shape, 0)
            key_pos = lax.broadcasted_iota(jnp.int32, scores.shape, 1)
            allowed = (key_pos <= query_pos) & (key_pos < length)
            scores = jnp.where(allowed, scores, masked_score)
            top = jnp.max(scores, axis=-1, keepdims=True)
            weights = jnp.exp(scores - top)
            total = jnp.sum(weights, axis=-1, keepdims=True)
            weighted = jnp.dot(
                weights.astype(jnp.bfloat16), values[:reach], preferred_element_type=jnp.float32
            )
            out_ref[pl.ds(row0, QROWS), cols] = (weighted / total).astype(jnp.bfloat16)


def attend(queries, keys, values, scales, length, first_head):
    seq, width = queries.shape
    heads = width // HD
    step_heads = 2 if heads % 2 == 0 and seq <= 512 else 1
    meta = jnp.stack((length, first_head)).astype(jnp.int32)
    spec = pl.BlockSpec((seq, step_heads * HD), lambda h: (0, h))
    smem = pl.BlockSpec(memory_space=pltpu.SMEM)
    return pl.pallas_call(
        functools.partial(attend_kernel, step_heads),
        grid=(heads // step_heads,),
        in_specs=[smem, smem, spec, spec, spec],
        out_specs=spec,
        out_shape=jax.ShapeDtypeStruct((seq, width), jnp.bfloat16),
        cost_estimate=pl.CostEstimate(
            flops=4 * seq * seq * width,
            bytes_accessed=8 * seq * width,
            transcendentals=seq * seq * heads,
        ),
    )(meta, scales, queries, keys, values)


def average_kernel(own_ref, peer_ref, tracker_ref, *rest):
    out_ref = rest[-1]
    out_ref[...] = (
        0.5 * (own_ref[...].astype(jnp.float32) + peer_ref[...].astype(jnp.float32))
        - step_size * tracker_ref[...].astype(jnp.float32)
    ).astype(jnp.bfloat16)


def average_rows(own, peer_rows, new_tracker, start, filled=None):
    rows, cols = peer_rows.shape
    tile = LAST_ROWS
    here = pl.BlockSpec((tile, cols), lambda i: (i + start // tile, 0))
    operands = [own, peer_rows, new_tracker]
    peer_spec = pl.BlockSpec((tile, cols), lambda i: (i, 0))
    if rows == tile:
        peer_spec = pl.BlockSpec(memory_space=pltpu.VMEM)
    specs = [here, peer_spec, here]
    aliases = {}
    if filled is not None:
        operands.append(filled)
        specs.append(pl.BlockSpec(memory_space=pl.ANY))
        aliases = {3: 0}
    return pl.pallas_call(
        average_kernel,
        grid=(rows // tile,),
        in_specs=specs,
        out_specs=here,
        out_shape=jax.ShapeDtypeStruct(own.shape, jnp.bfloat16),
        input_output_aliases=aliases,
        cost_estimate=pl.CostEstimate(
            flops=4 * rows * cols, bytes_accessed=8 * rows * cols, transcendentals=0
        ),
    )(*operands)


PAIR = 2
GROUP = PAIR * HD
MESH = pl.DeviceIdType.MESH


def scaled_rows(ref, scales, head, cols):
    return jnp.concatenate(
        [
            (
                ref[pl.ds(block * KBLK, KBLK), cols].astype(jnp.float32) * scales[block, head]
            ).astype(jnp.bfloat16)
            for block in range(ref.shape[0] // KBLK)
        ],
        axis=0,
    )


def attend_columns(queries, keys, values, allowed):
    scores = lax.dot_general(
        keys, queries, (((1,), (1,)), ((), ())), preferred_element_type=jnp.float32
    ) * (HD ** (-0.5))
    scores = jnp.where(allowed, scores, masked_score)
    top = jnp.max(scores, axis=0, keepdims=True)
    weights = jnp.exp(scores - top)
    total = jnp.sum(weights, axis=0, keepdims=True)
    return contract_rows(values, weights.astype(jnp.bfloat16)), top, total


def core_pair_kernel(
    length_ref, scales, query_hbm, key_hbm, value_hbm, grad_hbm, tracker_hbm, params_hbm, old_hbm,
    new_tracker_ref, new_params_ref,
    queries, keys, values, masked, tracker, params, old, peer_tracker, peer_params,
    peer_queries, low, high, part, stats, own, own_stats,
    load_sem, trade_send, trade_recv, query_send, query_recv, low_send, low_recv,
    high_send, high_recv, part_send, part_recv, stats_send, stats_recv,
):
    rows = queries.shape[0]
    groups = queries.shape[1] // GROUP
    side = lax.axis_index("ctx")
    place = lax.axis_index("dp")
    across = {"ctx": 1 - side}
    partner = {"dp": place + 1 - 2 * (place % 2)}
    length = length_ref[0]

    def span(group):
        return pl.ds(pl.multiple_of(group * GROUP, GROUP), GROUP)

    def remote(source, target, send, recv, device):
        return pltpu.make_async_remote_copy(
            src_ref=source, dst_ref=target, send_sem=send, recv_sem=recv,
            device_id=device, device_id_type=MESH,
        )

    def trade_tracker(group):
        here = span(group)
        return remote(tracker_hbm.at[here], peer_tracker.at[here],
                      trade_send.at[0, group], trade_recv.at[0, group], partner)

    def trade_params(group):
        here = span(group)
        return remote(params_hbm.at[here], peer_params.at[here],
                      trade_send.at[1, group], trade_recv.at[1, group], partner)

    def move_queries(group):
        here = span(group)
        return remote(query_hbm.at[:, here], peer_queries.at[:, here],
                      query_send.at[group], query_recv.at[group], across)

    def move_low(group):
        here = span(group)
        return remote(low.at[here], low.at[here], low_send.at[group], low_recv.at[group], across)

    def move_high(group):
        here = span(group)
        return remote(high.at[here], high.at[here], high_send.at[group], high_recv.at[group],
                      across)

    def move_part(group):
        here = span(group)
        return remote(part.at[here], part.at[here], part_send.at[group], part_recv.at[group],
                      across)

    def move_stats(group):
        return remote(stats.at[group], stats.at[group], stats_send.at[group],
                      stats_recv.at[group], across)

    loads = [
        pltpu.make_async_copy(source, target, load_sem.at[index])
        for index, (source, target) in enumerate((
            (query_hbm, queries), (key_hbm, keys), (value_hbm, values), (grad_hbm, masked),
            (tracker_hbm, tracker), (params_hbm, params), (old_hbm, old),
        ))
    ]
    for load in loads[:3]:
        load.start()
    barrier = pltpu.get_barrier_semaphore()
    for device in (across, partner):
        pl.semaphore_signal(barrier, inc=1, device_id=device, device_id_type=MESH)
    pl.semaphore_wait(barrier, 2)

    def each(first, last, body):
        def step(group, carry):
            body(group)
            return carry

        lax.fori_loop(first, last, step, 0)

    @pl.when(side == 1)
    def _():
        each(0, groups, lambda group: move_queries(group).start())

    def start_trades(group):
        trade_tracker(group).start()
        trade_params(group).start()

    each(0, groups, start_trades)
    for load in loads[3:]:
        load.start()
    for load in loads[:3]:
        load.wait()

    key_pos = lax.broadcasted_iota(jnp.int32, (rows, rows), 0)
    query_pos = lax.broadcasted_iota(jnp.int32, (rows, rows), 1)

    def heads_of(group):
        for local in range(PAIR):
            head = group * PAIR + local
            yield local, head, pl.ds(pl.multiple_of(head * HD, HD), HD)

    def own_keys(head, cols):
        return scaled_rows(keys, scales, head, cols), scaled_rows(values, scales, head, cols)

    def mask_grad():
        loads[3].wait()
        for block in range(masked.shape[0] // KBLK):
            here = pl.ds(block * KBLK, KBLK)
            position = block * KBLK + lax.broadcasted_iota(jnp.int32, (KBLK, masked.shape[1]), 0)
            masked[here] = jnp.where(
                position < length, masked[here].astype(jnp.float32), 0.0
            ).astype(jnp.bfloat16)

    def update(group):
        here = span(group)
        trade_tracker(group).wait_recv()
        trade_params(group).wait_recv()
        grad = jnp.dot(low[here], masked[pl.ds(0, rows)], preferred_element_type=jnp.float32)
        grad += jnp.dot(high[here], masked[pl.ds(rows, rows)], preferred_element_type=jnp.float32)
        new_tracker = (
            0.5 * (tracker[here].astype(jnp.float32) + peer_tracker[here].astype(jnp.float32))
            + grad
            - old[here].astype(jnp.float32)
        ).astype(jnp.bfloat16)
        new_tracker_ref[here] = new_tracker
        new_params_ref[here] = (
            0.5 * (params[here].astype(jnp.float32) + peer_params[here].astype(jnp.float32))
            - step_size * new_tracker.astype(jnp.float32)
        ).astype(jnp.bfloat16)

    def wait_rest():
        for load in loads[4:]:
            load.wait()

    @pl.when(side == 0)
    def _():
        causal = (key_pos <= query_pos) & (key_pos < length)
        live = key_pos < length

        def make_low(group):
            for _, head, cols in heads_of(group):
                head_keys, head_values = own_keys(head, cols)
                weighted, _, total = attend_columns(
                    queries[:, cols], head_keys, head_values, causal
                )
                low[cols] = (weighted / total).astype(jnp.bfloat16)

        def make_part(group):
            move_queries(group).wait_recv()
            for local, head, cols in heads_of(group):
                head_keys, head_values = own_keys(head, cols)
                weighted, top, total = attend_columns(
                    peer_queries[:, cols], head_keys, head_values, live
                )
                part[cols] = (weighted / total).astype(jnp.bfloat16)
                stats[group, pl.ds(local, 1)] = top
                stats[group, pl.ds(PAIR + local, 1)] = total

        def send_part(group):
            move_part(group).start()
            move_stats(group).start()

        def step(group):
            make_part(group)
            make_low(group + 1)
            send_part(group)

        make_low(0)
        move_low(0).start()
        each(0, groups - 1, step)
        make_part(groups - 1)
        mask_grad()
        send_part(groups - 1)
        each(1, groups, lambda group: move_low(group).start())
        wait_rest()

        def finish(group):
            move_high(group).wait_recv()
            update(group)

        each(0, groups, finish)

        def drain(group):
            move_low(group).wait_send()
            move_part(group).wait_send()
            move_stats(group).wait_send()

        each(0, groups, drain)

    @pl.when(side == 1)
    def _():
        causal = (key_pos <= query_pos) & (key_pos + rows < length)

        def make_own(group):
            for local, head, cols in heads_of(group):
                head_keys, head_values = own_keys(head, cols)
                weighted, top, total = attend_columns(
                    queries[:, cols], head_keys, head_values, causal
                )
                own[cols] = weighted
                own_stats[group, pl.ds(local, 1)] = top
                own_stats[group, pl.ds(PAIR + local, 1)] = total

        def make_high(group):
            move_part(group).wait_recv()
            move_stats(group).wait_recv()
            for local, _, cols in heads_of(group):
                part_top = stats[group, pl.ds(local, 1)]
                own_top = own_stats[group, pl.ds(local, 1)]
                top = jnp.maximum(part_top, own_top)
                part_share = jnp.exp(part_top - top) * stats[group, pl.ds(PAIR + local, 1)]
                own_share = jnp.exp(own_top - top)
                total = part_share + own_share * own_stats[group, pl.ds(PAIR + local, 1)]
                weighted = part[cols].astype(jnp.float32) * part_share + own[cols] * own_share
                high[cols] = (weighted / total).astype(jnp.bfloat16)

        def step(group):
            make_high(group)
            move_high(group - 1).start()

        each(0, groups, make_own)
        make_high(0)
        each(1, groups, step)
        mask_grad()
        move_high(groups - 1).start()
        wait_rest()

        def finish(group):
            move_low(group).wait_recv()
            update(group)

        each(0, groups, finish)

        def drain(group):
            move_queries(group).wait_send()
            move_high(group).wait_send()

        each(0, groups, drain)

    def drain_trades(group):
        trade_tracker(group).wait_send()
        trade_params(group).wait_send()

    each(0, groups, drain_trades)


def flush_kernel(tracker_ref, params_ref, tracker_out, params_out, sems):
    copies = [
        pltpu.make_async_copy(tracker_ref, tracker_out, sems.at[0]),
        pltpu.make_async_copy(params_ref, params_out, sems.at[1]),
    ]
    for copy in copies:
        copy.start()
    for copy in copies:
        copy.wait()


def flush(tracker, params):
    shape = jax.ShapeDtypeStruct(tracker.shape, tracker.dtype)
    return pl.pallas_call(
        flush_kernel,
        in_specs=[pl.BlockSpec(memory_space=pltpu.VMEM)] * 2,
        out_specs=[pl.BlockSpec(memory_space=pl.ANY)] * 2,
        out_shape=[shape, shape],
        scratch_shapes=[pltpu.SemaphoreType.DMA((2,))],
        compiler_params=pltpu.CompilerParams(vmem_limit_bytes=FLUSH_LIMIT),
        cost_estimate=pl.CostEstimate(
            flops=0, bytes_accessed=2 * tracker.nbytes, transcendentals=0
        ),
    )(tracker, params)


def core_pair_step(queries, keys, values, scales, length, out_grad, params, tracker, old_grad):
    rows, width = queries.shape
    cols = params.shape[1]
    groups = width // GROUP
    smem = pl.BlockSpec(memory_space=pltpu.SMEM)
    anywhere = pl.BlockSpec(memory_space=pl.ANY)
    whole = pl.BlockSpec(memory_space=pltpu.VMEM)
    square = pltpu.VMEM((width, cols), jnp.bfloat16)
    block = pltpu.VMEM((rows, width), jnp.bfloat16)
    turned = pltpu.VMEM((width, rows), jnp.bfloat16)
    stats = pltpu.VMEM((groups, 8, rows), jnp.float32)
    sems = pltpu.SemaphoreType.DMA
    shape = jax.ShapeDtypeStruct((width, cols), jnp.bfloat16)
    done = pl.pallas_call(
        core_pair_kernel,
        in_specs=[smem, smem] + [anywhere] * 7,
        out_specs=[whole, whole],
        out_shape=[shape, shape],
        scratch_shapes=[
            block, block, block, pltpu.VMEM(out_grad.shape, jnp.bfloat16),
            square, square, square, square, square,
            block, turned, turned, turned, stats,
            pltpu.VMEM((width, rows), jnp.float32), stats,
            sems((7,)), sems((2, groups)), sems((2, groups)),
        ] + [sems((groups,))] * 10,
        compiler_params=pltpu.CompilerParams(
            collective_id=0, has_side_effects=True, vmem_limit_bytes=VMEM_LIMIT
        ),
        cost_estimate=pl.CostEstimate(
            flops=4 * width * rows * cols + 12 * rows * rows * width,
            bytes_accessed=14 * width * cols,
            transcendentals=2 * rows * rows * width // HD,
        ),
    )(length.astype(jnp.int32)[None], scales, queries, keys, values, out_grad, tracker, params,
      old_grad)
    return flush(*done)


def step_with(bit_number):
    def step(
        queries, key_store, value_store, kv_exponents, valid_length,
        out_grad, params, tracker, old_grad,
    ):
        if bit_number == 0 and lax.axis_size("ctx") == 2:
            new_tracker, new_params = core_pair_step(
                queries[0], key_store[0], value_store[0],
                jnp.exp2(kv_exponents[0].astype(jnp.float32)), valid_length[0],
                out_grad[0], params[0], tracker[0], old_grad[0],
            )
            return (new_params[None], new_tracker[None])
        split = params.shape[1] - LAST_ROWS
        peer_tracker = from_partner(tracker[0], "dp", bit_number)
        peer_most = from_partner(params[0, :split], "dp", bit_number)
        peer_last = from_partner(params[0, split:], "dp", bit_number)
        length = valid_length[0]
        seq_rows = out_grad.shape[1]
        live_rows = jnp.arange(seq_rows)[:, None] < length
        masked = jnp.where(live_rows, out_grad[0], jnp.zeros((), jnp.bfloat16))
        groups = 2 if lax.axis_size("ctx") == 2 else 1
        exponents = gather_ctx(kv_exponents[0], 0)
        scales = jnp.exp2(exponents.astype(jnp.float32))
        pieces = []
        for group in range(groups):
            pieces.append(
                [
                    rows_to_heads(block[0], group, groups)
                    for block in (key_store, value_store, queries)
                ]
            )
        mine = lax.axis_index("ctx")
        group_heads = HEADS // (lax.axis_size("ctx") * groups)
        width = group_heads * HD
        own_parts = [
            attend(rows, keys, values, scales, length, (mine * groups + group) * group_heads)
            for group, (keys, values, rows) in enumerate(pieces)
        ]
        parts = [gather_ctx(own, 1) for own in own_parts]
        if groups == 1:
            attended = parts[0]
        else:
            attended = jnp.concatenate(
                [
                    part[:, side * width : (side + 1) * width]
                    for side in range(2)
                    for part in parts
                ],
                axis=1,
            )
        grad_new = contract_rows(attended, masked)
        tracker_sum = (
            0.5 * (tracker[0].astype(jnp.float32) + peer_tracker.astype(jnp.float32))
            + grad_new
            - old_grad[0].astype(jnp.float32)
        )
        new_tracker = tracker_sum.astype(jnp.bfloat16)
        new_params = average_rows(params[0], peer_most, new_tracker, 0)
        new_params = average_rows(params[0], peer_last, new_tracker, split, new_params)
        return (new_params[None], new_tracker[None])

    return step


def shards(
    queries,
    key_store,
    value_store,
    kv_exponents,
    valid_length,
    round_index,
    out_grad,
    params,
    tracker,
    old_grad,
):
    levels = lax.axis_size("dp").bit_length() - 1
    bit_now = round_index[0] % levels
    return lax.switch(
        bit_now,
        [step_with(bit_number) for bit_number in range(levels)],
        queries, key_store, value_store, kv_exponents, valid_length,
        out_grad, params, tracker, old_grad,
    )


def solution(mesh):
    placed = (
        P("dp", "ctx", None),
        P("dp", "ctx", None),
        P("dp", "ctx", None),
        P("dp", "ctx", None),
        P("dp"),
        P(),
        P("dp", None, "ctx"),
        P("dp", None, "ctx"),
        P("dp", None, "ctx"),
        P("dp", None, "ctx"),
    )
    return jax.shard_map(
        shards,
        mesh=mesh,
        in_specs=placed,
        out_specs=(P("dp", None, "ctx"), P("dp", None, "ctx")),
        check_vma=False,
    )
```

profile of v0, /device:TPU:0, one launch (start us, length us, event | category | flops | bytes accessed | tf_op | source)
XLA Modules:
  0.0 188.4 jit_solution(11568138081290273640)
XLA Ops:
  1.3 187.1 %conditional.1 = (bf16[2048,1024]{1,0:T(8,128)(2,1)}, bf16[2048,1024]{1,0:T(8,128)(2,1)}) conditional(s32[]{:T(128)} %clamp.3, (s32[1,2,16]{2,1,0:T(2,128)}, bf16[1,256,2048]{2,1,0:T(8,128)(2,1)}, bf16[1,256,2048]{2,1,0:T(8,128)(2,1)}, bf16[1,256,2048]{2,1,0:T(8,128)(2,1)}, bf16[1,512,1024]{2,1,0:T(8,128)(2,1)}, ...), branch_computations={%region_0.1_spmd, %region_1.2_spmd, %region_2.3_spmd, %region_3.4_... | conditional | flops 3758096384 | bytes 154144912 | solution.py:576
  1.5 3.0 %collective-permute-start.1 = (bf16[2048,1024]{1,0:T(8,128)(2,1)}, bf16[2048,1024]{1,0:T(8,128)(2,1)}, u32[]{:S(2)}, u32[]{:S(2)}) collective-permute-start(bf16[2048,1024]{1,0:T(8,128)(2,1)} %bitcast.173), channel_id=1, source_target_pairs={{0,4},{2,6},{4,0},{6,2},{8,12},{10,14},{12,8},{14,10},{16,20},{18,... | collective-permute-start | bytes 12582920 | tf_op jit(solution)/shard_map/cond/branch_1_fun/ppermute | solution.py:27
  4.5 1.5 collective-permute-start.2
  6.0 1.9 dynamic-slice_bitcast_fusion.5
  9.9 1.9 dynamic-slice_bitcast_fusion.4
  14.8 2.0 %dynamic-slice_bitcast_fusion.3 = (bf16[256,512]{1,0:T(8,128)(2,1)}, bf16[256,512]{1,0:T(8,128)(2,1)}) fusion(bf16[1,256,2048]{2,1,0:T(8,128)(2,1)} %get-tuple-element.91, s32[]{:T(128)S(6)} %select_n.244, s32[]{:T(128)S(6)} %select_n.253), kind=kLoop, calls=%fused_computation.41 | loop fusion | bytes 1048584 | tf_op jit(solution)/shard_map/cond/branch_1_fun/dynamic_slice | solution.py:59
  16.8 4.4 %slice_bitcast_fusion = bf16[1792,1024]{1,0:T(8,128)(2,1)} fusion(bf16[1,2048,1024]{2,1,0:T(8,128)(2,1)} %get-tuple-element.85), kind=kLoop, calls=%fused_computation.3 | loop fusion | bytes 7340032 | tf_op jit(solution)/shard_map/cond/branch_1_fun/squeeze | solution.py:512
  21.9 2.0 %collective-permute-start.8 = (bf16[256,512]{1,0:T(8,128)(2,1)}, bf16[256,512]{1,0:T(8,128)(2,1)S(1)}, u32[]{:S(2)}, u32[]{:S(2)}) collective-permute-start(bf16[256,512]{1,0:T(8,128)(2,1)} %get-tuple-element.139), channel_id=1, source_target_pairs={{0,1},{1,0},{2,3},{3,2},{4,5},{5,4},{6,7},{7,6},{8,9},{9,8},{10,11... | collective-permute-start | bytes 786440 | tf_op jit(solution)/shard_map/cond/branch_1_fun/ppermute | solution.py:37
  23.9 4.6 %collective-permute-done.4 = bf16[256,512]{1,0:T(8,128)(2,1)S(1)} collective-permute-done((bf16[256,512]{1,0:T(8,128)(2,1)}, bf16[256,512]{1,0:T(8,128)(2,1)S(1)}, u32[]{:S(2)}, u32[]{:S(2)}) %collective-permute-start.4) | collective-permute-done | bytes 262176 | tf_op jit(solution)/shard_map/cond/branch_1_fun/ppermute | solution.py:37
  29.7 2.0 %bitcast_select_fusion.13 = (bf16[256,512]{1,0:T(8,128)(2,1)S(1)}, bf16[256,512]{1,0:T(8,128)(2,1)S(1)}, bf16[256,512]{1,0:T(8,128)(2,1)S(1)}, bf16[256,512]{1,0:T(8,128)(2,1)}) fusion(bf16[256,512]{1,0:T(8,128)(2,1)} %collective-permute-done.3, pred[]{:T(512)S(6)} %eq.4, bf16[1,256,2048]{2,1,0:T(8,128)(2,1)S(1)} %copy-done.6, s32[]{:T(128)S(6)} %select_n.243, ...), kind=kLoop, calls=%fused_computation.37 | loop fusion | flops 524288 | bytes 2097161 | tf_op jit(solution)/shard_map/cond/branch_1_fun/jit(_where)/select_n | solution.py:43
  32.5 1.6 collective-permute-done.8
  34.1 5.6 %collective-permute-done.5 = bf16[256,512]{1,0:T(8,128)(2,1)S(1)} collective-permute-done((bf16[256,512]{1,0:T(8,128)(2,1)}, bf16[256,512]{1,0:T(8,128)(2,1)S(1)}, u32[]{:S(2)}, u32[]{:S(2)}) %collective-permute-start.5) | collective-permute-done | bytes 262176 | tf_op jit(solution)/shard_map/cond/branch_1_fun/ppermute | solution.py:37
  39.8 3.9 %collective-permute-done.9 = bf16[256,512]{1,0:T(8,128)(2,1)S(1)} collective-permute-done((bf16[256,512]{1,0:T(8,128)(2,1)}, bf16[256,512]{1,0:T(8,128)(2,1)S(1)}, u32[]{:S(2)}, u32[]{:S(2)}) %collective-permute-start.9) | collective-permute-done | bytes 262176 | tf_op jit(solution)/shard_map/cond/branch_1_fun/ppermute | solution.py:37
  43.7 2.1 %bitcast_select_fusion.9 = (bf16[256,512]{1,0:T(8,128)(2,1)S(1)}, bf16[256,512]{1,0:T(8,128)(2,1)S(1)}, bf16[256,512]{1,0:T(8,128)(2,1)S(1)}, bf16[256,512]{1,0:...) fusion(bf16[256,512]{1,0:T(8,128)(2,1)S(1)} %collective-permute, ...), kind=kLoop, calls=%fused_computation.33 | loop fusion | flops 1048576 | bytes 4194313 | tf_op jit(solution)/shard_map/cond/branch_1_fun/jit(_where)/select_n | solution.py:43
  47.5 4.6 %branch_1_fun.4 = bf16[512,512]{1,0:T(8,128)(2,1)} custom-call(s32[2]{0:T(128)} %pad_add_fusion.meta, f32[4,16]{1,0:T(4,128)} %fusion.14.scales, bf16[512,512]{1,0:T(8,128)(2,1)} %pad_maximum_fusion.q_ref, bf16[512,512]{1,0:T(8,128)(2,1)} %pad_maximum_fusion.1.k_ref, bf16[512,512]{1,0:T(8,128)(2,1)} %pad_maximum_fusion.2.v_ref), custom_call_target="tpu_custom_call" | custom-call | flops 536870912 | bytes 2097152 | tf_op jit(solution)/shard_map/cond/branch_1_fun/pallas_call | solution.py:111
  55.1 4.6 %branch_1_fun.5 = bf16[512,512]{1,0:T(8,128)(2,1)} custom-call(s32[2]{0:T(128)} %pad_add_fusion.1.meta, f32[4,16]{1,0:T(4,128)} %fusion.14.scales, bf16[512,512]{1,0:T(8,128)(2,1)} %pad_maximum_fusion.3.q_ref, bf16[512,512]{1,0:T(8,128)(2,1)} %pad_maximum_fusion.4.k_ref, bf16[512,512]{1,0:T(8,128)(2,1)} %pad_maximum_fusion.5.v_ref), custom_call_target="tpu_custom_call" | custom-call | flops 536870912 | bytes 2097152 | tf_op jit(solution)/shard_map/cond/branch_1_fun/pallas_call | solution.py:111
  63.5 3.7 %collective-permute-done.6 = bf16[512,512]{1,0:T(8,128)(2,1)} collective-permute-done((bf16[512,512]{1,0:T(8,128)(2,1)}, bf16[512,512]{1,0:T(8,128)(2,1)}, u32[]{:S(2)}, u32[]{:S(2)}) %collective-permute-start.6) | collective-permute-done | bytes 524320 | tf_op jit(solution)/shard_map/cond/branch_1_fun/ppermute | solution.py:37
  68.3 7.6 %collective-permute-done.10 = bf16[512,512]{1,0:T(8,128)(2,1)S(1)} collective-permute-done((bf16[512,512]{1,0:T(8,128)(2,1)}, bf16[512,512]{1,0:T(8,128)(2,1)S(1)}, u32[]{:S(2)}, u32[]{:S(2)}) %collective-permute-start.10) | collective-permute-done | bytes 524320 | tf_op jit(solution)/shard_map/cond/branch_1_fun/ppermute | solution.py:37
  77.0 19.3 %collective-permute-done.1 = bf16[2048,1024]{1,0:T(8,128)(2,1)} collective-permute-done((bf16[2048,1024]{1,0:T(8,128)(2,1)}, bf16[2048,1024]{1,0:T(8,128)(2,1)}, u32[]{:S(2)}, u32[]{:S(2)}) %collective-permute-start.1) | collective-permute-done | bytes 4194336 | tf_op jit(solution)/shard_map/cond/branch_1_fun/ppermute | solution.py:27
  96.3 8.1 %fusion.tracker_ref = bf16[2048,1024]{1,0:T(8,128)(2,1)} fusion(bf16[2048,1024]{1,0:T(8,128)(2,1)} %collective-permute-done.1, bf16[1,2048,1024]{2,1,0:T(8,128)(2,1)} %get-tuple-element.93, bf16[512,512]{1,0:T(8,128)(2,1)S(1)} %get-tuple-element.131, bf16[512,512]{1,0:T(8,128)(2,1)S(1)} %get-tuple-element.129, bf16[512,512]{1,0:T(8,128)(2,1)S(1)} %get-tuple-element.130, ...), kind=kOutput, calls=%fused_computation.2 | convolution fusion | flops 2173173760 | bytes 19923456 | tf_op jit(solution)/shard_map/cond/branch_1_fun/dot_general | solution.py:31
  104.4 70.5 %collective-permute-done.11.peer_ref = bf16[1792,1024]{1,0:T(8,128)(2,1)} collective-permute-done((bf16[1792,1024]{1,0:T(8,128)(2,1)}, bf16[1792,1024]{1,0:T(8,128)(2,1)}, u32[]{:S(2)}, u32[]{:S(2)}) %collective-permute-start.11) | collective-permute-done | bytes 3670048 | tf_op jit(solution)/shard_map/cond/branch_1_fun/ppermute | solution.py:27
  174.9 8.6 %branch_1_fun.6.rest_0_ = bf16[2048,1024]{1,0:T(8,128)(2,1)} custom-call(bf16[2048,1024]{1,0:T(8,128)(2,1)} %bitcast.163, bf16[1792,1024]{1,0:T(8,128)(2,1)} %collective-permute-done.11.peer_ref, bf16[2048,1024]{1,0:T(8,128)(2,1)} %fusion.tracker_ref), custom_call_target="tpu_custom_call" | custom-call | flops 7340032 | bytes 14680064 | tf_op jit(solution)/shard_map/cond/branch_1_fun/pallas_call | solution.py:147
  183.5 1.7 collective-permute-done.peer_ref
  186.0 2.4 %branch_1_fun.7 = bf16[2048,1024]{1,0:T(8,128)(2,1)} custom-call(bf16[2048,1024]{1,0:T(8,128)(2,1)} %bitcast.164, bf16[256,1024]{1,0:T(8,128)(2,1)} %copy-done.24, bf16[2048,1024]{1,0:T(8,128)(2,1)} %fusion.tracker_ref, bf16[2048,1024]{1,0:T(8,128)(2,1)} %branch_1_fun.6.rest_0_), custom_call_target="tpu_custom_call", output_to_operand_aliasing={{}: (3, {})} | custom-call | flops 1048576 | bytes 2097152 | tf_op jit(solution)/shard_map/cond/branch_1_fun/pallas_call | solution.py:147
  (48 shorter events, 19.4 us)
Async XLA Ops:
  1.5 94.8 %collective-permute-start.1 = (bf16[2048,1024]{1,0:T(8,128)(2,1)}, bf16[2048,1024]{1,0:T(8,128)(2,1)}, u32[]{:S(2)}, u32[]{:S(2)}) collective-permute-start(bf16[2048,1024]{1,0:T(8,128)(2,1)} %bitcast.173), channel_id=1, source_target_pairs={{0,4},{2,6},{4,0},{6,2},{8,12},{10,14},{12,8},{14,10},{16,20},{18,... | collective-permute-start | bytes 12582920 | tf_op jit(solution)/shard_map/cond/branch_1_fun/ppermute | solution.py:27
  4.5 16.6 %collective-permute-start.2 = (s32[2,16]{1,0:T(2,128)}, s32[2,16]{1,0:T(2,128)S(1)}, u32[]{:S(2)}, u32[]{:S(2)}) collective-permute-start(s32[2,16]{1,0:T(2,128)} %bitcast.178), channel_id=1, source_target_pairs={{0,1},{1,0},{2,3},{3,2},{4,5},{5,4},{6,7},{7,6},{8,9},{9,8},{10,11... | collective-permute-start | bytes 392 | tf_op jit(solution)/shard_map/cond/branch_1_fun/ppermute | solution.py:37
  7.9 14.0 %collective-permute-start.3 = (bf16[256,512]{1,0:T(8,128)(2,1)}, bf16[256,512]{1,0:T(8,128)(2,1)}, u32[]{:S(2)}, u32[]{:S(2)}) collective-permute-start(bf16[256,512]{1,0:T(8,128)(2,1)} %get-tuple-element.142), channel_id=1, source_target_pairs={{0,1},{1,0},{2,3},{3,2},{4,5},{5,4},{6,7},{7,6},{8,9},{9,8},{10,11... | collective-permute-start | bytes 786440 | tf_op jit(solution)/shard_map/cond/branch_1_fun/ppermute | solution.py:37
  8.4 15.5 %collective-permute-start.7 = (bf16[256,512]{1,0:T(8,128)(2,1)}, bf16[256,512]{1,0:T(8,128)(2,1)}, u32[]{:S(2)}, u32[]{:S(2)}) collective-permute-start(bf16[256,512]{1,0:T(8,128)(2,1)} %get-tuple-element.143), channel_id=1, source_target_pairs={{0,1},{1,0},{2,3},{3,2},{4,5},{5,4},{6,7},{7,6},{8,9},{9,8},{10,11... | collective-permute-start | bytes 786440 | tf_op jit(solution)/shard_map/cond/branch_1_fun/ppermute | solution.py:37
  11.8 16.7 %collective-permute-start.4 = (bf16[256,512]{1,0:T(8,128)(2,1)}, bf16[256,512]{1,0:T(8,128)(2,1)S(1)}, u32[]{:S(2)}, u32[]{:S(2)}) collective-permute-start(bf16[256,512]{1,0:T(8,128)(2,1)} %get-tuple-element.138), channel_id=1, source_target_pairs={{0,1},{1,0},{2,3},{3,2},{4,5},{5,4},{6,7},{7,6},{8,9},{9,8},{10,11... | collective-permute-start | bytes 786440 | tf_op jit(solution)/shard_map/cond/branch_1_fun/ppermute | solution.py:37
  14.8 6.5 %copy-start.30 = (s32[1,2,16]{2,1,0:T(2,128)S(1)}, s32[1,2,16]{2,1,0:T(2,128)}, u32[]{:S(2)}) copy-start(s32[1,2,16]{2,1,0:T(2,128)} %get-tuple-element.88) | copy-start | bytes 388 | tf_op jit(solution)/shard_map/cond
  14.8 14.9 %copy-start.6 = (bf16[1,256,2048]{2,1,0:T(8,128)(2,1)S(1)}, bf16[1,256,2048]{2,1,0:T(8,128)(2,1)}, u32[]{:S(2)}) copy-start(bf16[1,256,2048]{2,1,0:T(8,128)(2,1)} %get-tuple-element.89) | copy-start | bytes 3145732 | tf_op jit(solution)/shard_map/cond
  16.8 26.9 %copy-start = (bf16[1,256,2048]{2,1,0:T(8,128)(2,1)S(1)}, bf16[1,256,2048]{2,1,0:T(8,128)(2,1)}, u32[]{:S(2)}) copy-start(bf16[1,256,2048]{2,1,0:T(8,128)(2,1)} %get-tuple-element.90) | copy-start | bytes 3145732 | tf_op jit(solution)/shard_map/cond
  16.8 26.9 %copy-start.3 = (bf16[1,256,2048]{2,1,0:T(8,128)(2,1)S(1)}, bf16[1,256,2048]{2,1,0:T(8,128)(2,1)}, u32[]{:S(2)}) copy-start(bf16[1,256,2048]{2,1,0:T(8,128)(2,1)} %get-tuple-element.91) | copy-start | bytes 3145732 | tf_op jit(solution)/shard_map/cond
  21.2 153.7 %collective-permute-start.11 = (bf16[1792,1024]{1,0:T(8,128)(2,1)}, bf16[1792,1024]{1,0:T(8,128)(2,1)}, u32[]{:S(2)}, u32[]{:S(2)}) collective-permute-start(bf16[1792,1024]{1,0:T(8,128)(2,1)} %slice_bitcast_fusion), channel_id=1, source_target_pairs={{0,4},{2,6},{4,0},{6,2},{8,12},{10,14},{12,8},{14,10},{16,20},{18,... | collective-permute-start | bytes 11010056 | tf_op jit(solution)/shard_map/cond/branch_1_fun/ppermute | solution.py:27
  21.9 12.3 %collective-permute-start.8 = (bf16[256,512]{1,0:T(8,128)(2,1)}, bf16[256,512]{1,0:T(8,128)(2,1)S(1)}, u32[]{:S(2)}, u32[]{:S(2)}) collective-permute-start(bf16[256,512]{1,0:T(8,128)(2,1)} %get-tuple-element.139), channel_id=1, source_target_pairs={{0,1},{1,0},{2,3},{3,2},{4,5},{5,4},{6,7},{7,6},{8,9},{9,8},{10,11... | collective-permute-start | bytes 786440 | tf_op jit(solution)/shard_map/cond/branch_1_fun/ppermute | solution.py:37
  23.9 15.9 %collective-permute-start.5 = (bf16[256,512]{1,0:T(8,128)(2,1)}, bf16[256,512]{1,0:T(8,128)(2,1)S(1)}, u32[]{:S(2)}, u32[]{:S(2)}) collective-permute-start(bf16[256,512]{1,0:T(8,128)(2,1)} %get-tuple-element.134), channel_id=1, source_target_pairs={{0,1},{1,0},{2,3},{3,2},{4,5},{5,4},{6,7},{7,6},{8,9},{9,8},{10,11... | collective-permute-start | bytes 786440 | tf_op jit(solution)/shard_map/cond/branch_1_fun/ppermute | solution.py:37
  28.5 0.7 copy-start.27
  29.2 14.5 %collective-permute-start.9 = (bf16[256,512]{1,0:T(8,128)(2,1)}, bf16[256,512]{1,0:T(8,128)(2,1)S(1)}, u32[]{:S(2)}, u32[]{:S(2)}) collective-permute-start(bf16[256,512]{1,0:T(8,128)(2,1)} %get-tuple-element.135), channel_id=1, source_target_pairs={{0,1},{1,0},{2,3},{3,2},{4,5},{5,4},{6,7},{7,6},{8,9},{9,8},{10,11... | collective-permute-start | bytes 786440 | tf_op jit(solution)/shard_map/cond/branch_1_fun/ppermute | solution.py:37
  32.5 20.1 %copy-start.18 = (bf16[256,512]{1,0:T(8,128)(2,1)S(1)}, bf16[256,512]{1,0:T(8,128)(2,1)}, u32[]{:S(2)}) copy-start(bf16[256,512]{1,0:T(8,128)(2,1)} %get-tuple-element.141) | copy-start | bytes 786436 | tf_op jit(solution)/shard_map/cond
  45.8 7.6 %copy-start.21 = (bf16[256,512]{1,0:T(8,128)(2,1)S(1)}, bf16[256,512]{1,0:T(8,128)(2,1)}, u32[]{:S(2)}) copy-start(bf16[256,512]{1,0:T(8,128)(2,1)} %get-tuple-element.133) | copy-start | bytes 786436 | tf_op jit(solution)/shard_map/cond
  52.1 15.1 %copy-start.12 = (bf16[512,512]{1,0:T(8,128)(2,1)S(1)}, bf16[512,512]{1,0:T(8,128)(2,1)}, u32[]{:S(2)}) copy-start(bf16[512,512]{1,0:T(8,128)(2,1)} %branch_1_fun.4) | copy-start | bytes 1572868 | tf_op jit(solution)/shard_map/cond
  52.1 15.1 %collective-permute-start.6 = (bf16[512,512]{1,0:T(8,128)(2,1)}, bf16[512,512]{1,0:T(8,128)(2,1)}, u32[]{:S(2)}, u32[]{:S(2)}) collective-permute-start(bf16[512,512]{1,0:T(8,128)(2,1)} %branch_1_fun.4), channel_id=1, source_target_pairs={{0,1},{1,0},{2,3},{3,2},{4,5},{5,4},{6,7},{7,6},{8,9},{9,8},{10,11... | collective-permute-start | bytes 1572872 | tf_op jit(solution)/shard_map/cond/branch_1_fun/ppermute | solution.py:37
  54.2 42.0 %copy-start.15 = (bf16[1,512,1024]{2,1,0:T(8,128)(2,1)S(1)}, bf16[1,512,1024]{2,1,0:T(8,128)(2,1)}, u32[]{:S(2)}) copy-start(bf16[1,512,1024]{2,1,0:T(8,128)(2,1)} %get-tuple-element.92) | copy-start | bytes 3145732 | tf_op jit(solution)/shard_map/cond
  59.7 36.6 %copy-start.9 = (bf16[1,2048,1024]{2,1,0:T(8,128)(2,1)S(1)}, bf16[1,2048,1024]{2,1,0:T(8,128)(2,1)}, u32[]{:S(2)}) copy-start(bf16[1,2048,1024]{2,1,0:T(8,128)(2,1)} %get-tuple-element.86) | copy-start | bytes 12582916 | tf_op jit(solution)/shard_map/cond
  59.7 16.2 %collective-permute-start.10 = (bf16[512,512]{1,0:T(8,128)(2,1)}, bf16[512,512]{1,0:T(8,128)(2,1)S(1)}, u32[]{:S(2)}, u32[]{:S(2)}) collective-permute-start(bf16[512,512]{1,0:T(8,128)(2,1)} %branch_1_fun.5), channel_id=1, source_target_pairs={{0,1},{1,0},{2,3},{3,2},{4,5},{5,4},{6,7},{7,6},{8,9},{9,8},{10,11... | collective-permute-start | bytes 1572872 | tf_op jit(solution)/shard_map/cond/branch_1_fun/ppermute | solution.py:37
  62.3 122.9 %collective-permute-start = (bf16[256,1024]{1,0:T(8,128)(2,1)S(1)}, bf16[256,1024]{1,0:T(8,128)(2,1)S(1)}, u32[]{:S(2)}, u32[]{:S(2)}) collective-permute-start(bf16[256,1024]{1,0:T(8,128)(2,1)S(1)} %slice_bitcast_fusion.1), channel_id=1, source_target_pairs={{0,4},{2,6},{4,0},{6,2},{8,12},{10,14},{12,8},{14,10},{16,20},{18,... | collective-permute-start | bytes 1572872 | tf_op jit(solution)/shard_map/cond/branch_1_fun/ppermute | solution.py:27
  185.2 0.8 copy-start.24
where the time goes:
time: 189 us; the launch traced here: 188 us
  waiting for transfers between devices  118 us (62%)
  Pallas kernels  20.2 us (11%)
  other arithmetic  15 us (8%)
  local copies, waits for them, and re-layouts  12.7 us (7%)
  starting transfers between devices  12.3 us (7%)
  matrix products  8.15 us (4%)
    ppermute x3, waiting for transfers between devices, from_partner(): return lax.ppermute(value, axis, pairs)  91.5 us
    ppermute x9, waiting for transfers between devices, from_other(): return lax.ppermute(block, 'ctx', [(0, 1), (1, 0)])  27 us
    pallas_call x2, Pallas kernels, average_rows(): pl.pallas_call(average_kernel, grid=(rows // tile,), in_specs=specs, out_...  11 us
    pallas_call x2, Pallas kernels, attend(): pl.pallas_call(functools.partial(attend_kernel, step_heads), grid=(heads...  9.18 us
    ppermute x9, starting transfers between devices, from_other(): return lax.ppermute(block, 'ctx', [(0, 1), (1, 0)])  8.63 us
    dot_general x1, matrix products, contract_rows(): lax.dot_general(left_rows, right_rows, (((0,), (0,)), ((), ())), preferre...  8.15 us
    select_n x5, other arithmetic, in_order(): jnp.where(first, own, other)  6.32 us
    dynamic_slice x3, local copies, waits for them, and re-layouts, rows_to_heads(): lax.dynamic_slice_in_dim(block, ((1 - mine) * groups + group) * width, wi...  5.7 us
  transfers between devices with their start and end apart: 12, of which 9 were waited for; matrix products, arithmetic and copies ran while one was open for 18% of the time, Pallas kernels for 9%

commit v1 on v0

--- a/solution.py
+++ b/solution.py
@@ -12,9 +12,11 @@
 HD = 128
 KBLK = 128
 QROWS = 256
-LAST_ROWS = 256
+PIECES = ((384, 384), (64, 64), (64, 64))
+MOST_TILE = 256
 VMEM_LIMIT = 40 * 2**20
 FLUSH_LIMIT = 16 * 2**20
+AVERAGE_LIMIT = 16 * 2**20
 
 
 step_size = 0.1
@@ -130,14 +132,11 @@
     ).astype(jnp.bfloat16)
 
 
-def average_rows(own, peer_rows, new_tracker, start, filled=None):
+def average_rows(own, peer_rows, new_tracker, start, tile, filled=None):
     rows, cols = peer_rows.shape
-    tile = LAST_ROWS
     here = pl.BlockSpec((tile, cols), lambda i: (i + start // tile, 0))
     operands = [own, peer_rows, new_tracker]
     peer_spec = pl.BlockSpec((tile, cols), lambda i: (i, 0))
-    if rows == tile:
-        peer_spec = pl.BlockSpec(memory_space=pltpu.VMEM)
     specs = [here, peer_spec, here]
     aliases = {}
     if filled is not None:
@@ -151,6 +150,7 @@
         out_specs=here,
         out_shape=jax.ShapeDtypeStruct(own.shape, jnp.bfloat16),
         input_output_aliases=aliases,
+        compiler_params=pltpu.CompilerParams(vmem_limit_bytes=AVERAGE_LIMIT),
         cost_estimate=pl.CostEstimate(
             flops=4 * rows * cols, bytes_accessed=8 * rows * cols, transcendentals=0
         ),
@@ -162,11 +162,16 @@
 MESH = pl.DeviceIdType.MESH
 
 
+def power_of_two(exponent):
+    return jnp.where(exponent > 0, 2.0, jnp.where(exponent < 0, 0.5, 1.0)).astype(jnp.float32)
+
+
 def scaled_rows(ref, scales, head, cols):
     return jnp.concatenate(
         [
             (
-                ref[pl.ds(block * KBLK, KBLK), cols].astype(jnp.float32) * scales[block, head]
+                ref[pl.ds(block * KBLK, KBLK), cols].astype(jnp.float32)
+                * power_of_two(scales[block, head])
             ).astype(jnp.bfloat16)
             for block in range(ref.shape[0] // KBLK)
         ],
@@ -189,7 +194,7 @@
     length_ref, scales, query_hbm, key_hbm, value_hbm, grad_hbm, tracker_hbm, params_hbm, old_hbm,
     new_tracker_ref, new_params_ref,
     queries, keys, values, masked, tracker, params, old, peer_tracker, peer_params,
-    peer_queries, low, high, part, stats, own, own_stats,
+    peer_queries, low, high, part, stats, own, own_stats, base, average,
     load_sem, trade_send, trade_recv, query_send, query_recv, low_send, low_recv,
     high_send, high_recv, part_send, part_recv, stats_send, stats_recv,
 ):
@@ -255,7 +260,6 @@
     barrier = pltpu.get_barrier_semaphore()
     for device in (across, partner):
         pl.semaphore_signal(barrier, inc=1, device_id=device, device_id_type=MESH)
-    pl.semaphore_wait(barrier, 2)
 
     def each(first, last, body):
         def step(group, carry):
@@ -264,20 +268,6 @@
 
         lax.fori_loop(first, last, step, 0)
 
-    @pl.when(side == 1)
-    def _():
-        each(0, groups, lambda group: move_queries(group).start())
-
-    def start_trades(group):
-        trade_tracker(group).start()
-        trade_params(group).start()
-
-    each(0, groups, start_trades)
-    for load in loads[3:]:
-        load.start()
-    for load in loads[:3]:
-        load.wait()
-
     key_pos = lax.broadcasted_iota(jnp.int32, (rows, rows), 0)
     query_pos = lax.broadcasted_iota(jnp.int32, (rows, rows), 1)
 
@@ -288,6 +278,9 @@
 
     def own_keys(head, cols):
         return scaled_rows(keys, scales, head, cols), scaled_rows(values, scales, head, cols)
+
+    def lanes(index):
+        return pl.ds(index * rows, rows)
 
     def mask_grad():
         loads[3].wait()
@@ -298,39 +291,74 @@
                 position < length, masked[here].astype(jnp.float32), 0.0
             ).astype(jnp.bfloat16)
 
-    def update(group):
+    def grad_part(block, group, first_row):
+        return jnp.dot(
+            block[span(group)], masked[pl.ds(first_row, rows)], preferred_element_type=jnp.float32
+        )
+
+    def update(group, known, known_row, arriving, arriving_row, arrival):
         here = span(group)
         trade_tracker(group).wait_recv()
         trade_params(group).wait_recv()
-        grad = jnp.dot(low[here], masked[pl.ds(0, rows)], preferred_element_type=jnp.float32)
-        grad += jnp.dot(high[here], masked[pl.ds(rows, rows)], preferred_element_type=jnp.float32)
-        new_tracker = (
+        base[...] = (
             0.5 * (tracker[here].astype(jnp.float32) + peer_tracker[here].astype(jnp.float32))
-            + grad
+            + grad_part(known, group, known_row)
             - old[here].astype(jnp.float32)
-        ).astype(jnp.bfloat16)
+        )
+        average[...] = 0.5 * (
+            params[here].astype(jnp.float32) + peer_params[here].astype(jnp.float32)
+        )
+        arrival.wait_recv()
+        new_tracker = (base[...] + grad_part(arriving, group, arriving_row)).astype(jnp.bfloat16)
         new_tracker_ref[here] = new_tracker
         new_params_ref[here] = (
-            0.5 * (params[here].astype(jnp.float32) + peer_params[here].astype(jnp.float32))
-            - step_size * new_tracker.astype(jnp.float32)
+            average[...] - step_size * new_tracker.astype(jnp.float32)
         ).astype(jnp.bfloat16)
 
     def wait_rest():
         for load in loads[4:]:
             load.wait()
 
+    def make_low(group):
+        for _, head, cols in heads_of(group):
+            head_keys, head_values = own_keys(head, cols)
+            weighted, _, total = attend_columns(
+                queries[:, cols], head_keys, head_values, (key_pos <= query_pos) & (key_pos < length)
+            )
+            low[cols] = (weighted / total).astype(jnp.bfloat16)
+
     @pl.when(side == 0)
     def _():
-        causal = (key_pos <= query_pos) & (key_pos < length)
+        for load in loads[:3]:
+            load.wait()
+        make_low(0)
+
+    pl.semaphore_wait(barrier, 2)
+
+    @pl.when(side == 0)
+    def _():
+        move_low(0).start()
+
+    @pl.when(side == 1)
+    def _():
+        each(0, groups, lambda group: move_queries(group).start())
+
+    def start_trades(group):
+        trade_tracker(group).start()
+        trade_params(group).start()
+
+    each(0, groups, start_trades)
+    for load in loads[3:]:
+        load.start()
+
+    @pl.when(side == 1)
+    def _():
+        for load in loads[:3]:
+            load.wait()
+
+    @pl.when(side == 0)
+    def _():
         live = key_pos < length
-
-        def make_low(group):
-            for _, head, cols in heads_of(group):
-                head_keys, head_values = own_keys(head, cols)
-                weighted, _, total = attend_columns(
-                    queries[:, cols], head_keys, head_values, causal
-                )
-                low[cols] = (weighted / total).astype(jnp.bfloat16)
 
         def make_part(group):
             move_queries(group).wait_recv()
@@ -340,8 +368,8 @@
                     peer_queries[:, cols], head_keys, head_values, live
                 )
                 part[cols] = (weighted / total).astype(jnp.bfloat16)
-                stats[group, pl.ds(local, 1)] = top
-                stats[group, pl.ds(PAIR + local, 1)] = total
+                stats[group, :, lanes(local)] = top
+                stats[group, :, lanes(PAIR + local)] = total
 
         def send_part(group):
             move_part(group).start()
@@ -349,21 +377,22 @@
 
         def step(group):
             make_part(group)
-            make_low(group + 1)
+            make_low(group + 2)
             send_part(group)
 
-        make_low(0)
-        move_low(0).start()
-        each(0, groups - 1, step)
+        make_low(1)
+        move_low(1).start()
+        each(0, groups - 2, step)
+        make_part(groups - 2)
+        send_part(groups - 2)
         make_part(groups - 1)
         mask_grad()
         send_part(groups - 1)
-        each(1, groups, lambda group: move_low(group).start())
+        each(2, groups, lambda group: move_low(group).start())
         wait_rest()
 
         def finish(group):
-            move_high(group).wait_recv()
-            update(group)
+            update(group, low, 0, high, rows, move_high(group))
 
         each(0, groups, finish)
 
@@ -385,19 +414,19 @@
                     queries[:, cols], head_keys, head_values, causal
                 )
                 own[cols] = weighted
-                own_stats[group, pl.ds(local, 1)] = top
-                own_stats[group, pl.ds(PAIR + local, 1)] = total
+                own_stats[group, :, lanes(local)] = top
+                own_stats[group, :, lanes(PAIR + local)] = total
 
         def make_high(group):
             move_part(group).wait_recv()
             move_stats(group).wait_recv()
             for local, _, cols in heads_of(group):
-                part_top = stats[group, pl.ds(local, 1)]
-                own_top = own_stats[group, pl.ds(local, 1)]
+                part_top = stats[group, :, lanes(local)]
+                own_top = own_stats[group, :, lanes(local)]
                 top = jnp.maximum(part_top, own_top)
-                part_share = jnp.exp(part_top - top) * stats[group, pl.ds(PAIR + local, 1)]
+                part_share = jnp.exp(part_top - top) * stats[group, :, lanes(PAIR + local)]
                 own_share = jnp.exp(own_top - top)
-                total = part_share + own_share * own_stats[group, pl.ds(PAIR + local, 1)]
+                total = part_share + own_share * own_stats[group, :, lanes(PAIR + local)]
                 weighted = part[cols].astype(jnp.float32) * part_share + own[cols] * own_share
                 high[cols] = (weighted / total).astype(jnp.bfloat16)
 
@@ -413,8 +442,7 @@
         wait_rest()
 
         def finish(group):
-            move_low(group).wait_recv()
-            update(group)
+            update(group, high, rows, low, 0, move_low(group))
 
         each(0, groups, finish)
 
@@ -467,7 +495,7 @@
     square = pltpu.VMEM((width, cols), jnp.bfloat16)
     block = pltpu.VMEM((rows, width), jnp.bfloat16)
     turned = pltpu.VMEM((width, rows), jnp.bfloat16)
-    stats = pltpu.VMEM((groups, 8, rows), jnp.float32)
+    stats = pltpu.VMEM((groups, 1, 2 * PAIR * rows), jnp.float32)
     sems = pltpu.SemaphoreType.DMA
     shape = jax.ShapeDtypeStruct((width, cols), jnp.bfloat16)
     done = pl.pallas_call(
@@ -480,6 +508,7 @@
             square, square, square, square, square,
             block, turned, turned, turned, stats,
             pltpu.VMEM((width, rows), jnp.float32), stats,
+            pltpu.VMEM((GROUP, cols), jnp.float32), pltpu.VMEM((GROUP, cols), jnp.float32),
             sems((7,)), sems((2, groups)), sems((2, groups)),
         ] + [sems((groups,))] * 10,
         compiler_params=pltpu.CompilerParams(
@@ -503,14 +532,22 @@
         if bit_number == 0 and lax.axis_size("ctx") == 2:
             new_tracker, new_params = core_pair_step(
                 queries[0], key_store[0], value_store[0],
-                jnp.exp2(kv_exponents[0].astype(jnp.float32)), valid_length[0],
+                kv_exponents[0], valid_length[0],
                 out_grad[0], params[0], tracker[0], old_grad[0],
             )
             return (new_params[None], new_tracker[None])
-        split = params.shape[1] - LAST_ROWS
+        pieces_at = []
+        start = params.shape[1] - sum(rows for rows, _ in PIECES)
+        pieces_at.append((0, start, MOST_TILE))
+        for rows, tile in PIECES:
+            pieces_at.append((start, rows, tile))
+            start += rows
         peer_tracker = from_partner(tracker[0], "dp", bit_number)
-        peer_most = from_partner(params[0, :split], "dp", bit_number)
-        peer_last = from_partner(params[0, split:], "dp", bit_number)
+        peer_pieces = []
+        for start, rows, _ in pieces_at:
+            peer_pieces.append(
+                from_partner(params[0, start : start + rows], "dp", bit_number)
+            )
         length = valid_length[0]
         seq_rows = out_grad.shape[1]
         live_rows = jnp.arange(seq_rows)[:, None] < length
@@ -552,8 +589,9 @@
             - old_grad[0].astype(jnp.float32)
         )
         new_tracker = tracker_sum.astype(jnp.bfloat16)
-        new_params = average_rows(params[0], peer_most, new_tracker, 0)
-        new_params = average_rows(params[0], peer_last, new_tracker, split, new_params)
+        new_params = None
+        for (start, _, tile), peer_rows in zip(pieces_at, peer_pieces):
+            new_params = average_rows(params[0], peer_rows, new_tracker, start, tile, new_params)
         return (new_params[None], new_tracker[None])
 
     return step

time: 189 us -> 192 us (1.016)
  other arithmetic: 15 us -> 17.8 us
  starting transfers between devices: 12.3 us -> 15 us
  waiting for transfers between devices: 118 us -> 116 us
    ppermute x9, waiting for transfers between devices: 27 us -> 22.2 us  [from_other(): return lax.ppermute(block, 'ctx', [(0, 1), (1, 0)])]
    concatenate x6, other arithmetic: 4.97 us -> 8.04 us  [in_order(): jnp.concatenate((jnp.where(first, own, other), jnp.where(first, other, ow...]
    ppermute x3 -> x5, waiting for transfers between devices: 91.5 us -> 93.8 us  [from_partner(): return lax.ppermute(value, axis, pairs)]
    ppermute x3 -> x5, starting transfers between devices: 3.72 us -> 5.23 us  [from_partner(): return lax.ppermute(value, axis, pairs)]
    squeeze x2 -> x3, local copies, waits for them, and re-layouts: 5.47 us -> 6.75 us  [step(): params[0, start:start + rows]]
    pallas_call x2 -> x4, Pallas kernels: 11 us -> 11.6 us  [average_rows(): pl.pallas_call(average_kernel, grid=(rows // tile,), in_specs=specs, out_...]
  transfers between devices with their start and end apart: 12 -> 14, of which waited for: 9 -> 8; matrix products, arithmetic and copies ran while one was open for 18% -> 20% of each run, Pallas kernels for 9% -> 10%
where the time goes in v1:
time: 192 us; the launch traced here: 191 us
  waiting for transfers between devices  116 us (60%)
  Pallas kernels  20.9 us (11%)
  other arithmetic  17.8 us (9%)
  starting transfers between devices  15 us (8%)
  local copies, waits for them, and re-layouts  11.5 us (6%)
  matrix products  8.31 us (4%)
    ppermute x5, waiting for transfers between devices, from_partner(): return lax.ppermute(value, axis, pairs)  93.8 us
    ppermute x9, waiting for transfers between devices, from_other(): return lax.ppermute(block, 'ctx', [(0, 1), (1, 0)])  22.2 us
    pallas_call x4, Pallas kernels, average_rows(): pl.pallas_call(average_kernel, grid=(rows // tile,), in_specs=specs, out_...  11.6 us
    ppermute x9, starting transfers between devices, from_other(): return lax.ppermute(block, 'ctx', [(0, 1), (1, 0)])  9.75 us
    pallas_call x2, Pallas kernels, attend(): pl.pallas_call(functools.partial(attend_kernel, step_heads), grid=(heads...  9.23 us
    dot_general x1, matrix products, contract_rows(): lax.dot_general(left_rows, right_rows, (((0,), (0,)), ((), ())), preferre...  8.31 us
    concatenate x6, other arithmetic, in_order(): jnp.concatenate((jnp.where(first, own, other), jnp.where(first, other, ow...  8.04 us
    squeeze x3, local copies, waits for them, and re-layouts, step(): params[0, start:start + rows]  6.75 us
  transfers between devices with their start and end apart: 14, of which 8 were waited for; matrix products, arithmetic and copies ran while one was open for 20% of the time, Pallas kernels for 10%

profile of v1, /device:TPU:0, one launch (start us, length us, event | category | flops | bytes accessed | tf_op | source)
XLA Modules:
  0.0 191.0 jit_solution(14727107760217010497)
XLA Ops:
  1.3 189.6 %conditional.1 = (bf16[2048,1024]{1,0:T(8,128)(2,1)}, bf16[2048,1024]{1,0:T(8,128)(2,1)}) conditional(s32[]{:T(128)} %clamp.3, (s32[1,2,16]{2,1,0:T(2,128)}, bf16[1,256,2048]{2,1,0:T(8,128)(2,1)}, bf16[1,256,2048]{2,1,0:T(8,128)(2,1)}, bf16[1,256,2048]{2,1,0:T(8,128)(2,1)}, bf16[1,512,1024]{2,1,0:T(8,128)(2,1)}, ...), branch_computations={%region_0.1_spmd, %region_1.2_spmd, %region_2.3_spmd, %region_3.4_... | conditional | flops 3758096384 | bytes 155717712 | solution.py:614
  1.5 3.0 %collective-permute-start.1 = (bf16[2048,1024]{1,0:T(8,128)(2,1)}, bf16[2048,1024]{1,0:T(8,128)(2,1)}, u32[]{:S(2)}, u32[]{:S(2)}) collective-permute-start(bf16[2048,1024]{1,0:T(8,128)(2,1)} %bitcast.190), channel_id=1, source_target_pairs={{0,4},{2,6},{4,0},{6,2},{8,12},{10,14},{12,8},{14,10},{16,20},{18,... | collective-permute-start | bytes 12582920 | tf_op jit(solution)/shard_map/cond/branch_1_fun/ppermute | solution.py:29
  9.2 1.8 dynamic-slice_bitcast_fusion.4
  14.7 1.9 dynamic-slice_bitcast_fusion.3
  16.5 1.7 slice_bitcast_fusion.2
  18.2 3.9 %slice_bitcast_fusion = bf16[1536,1024]{1,0:T(8,128)(2,1)} fusion(bf16[1,2048,1024]{2,1,0:T(8,128)(2,1)} %get-tuple-element.85), kind=kLoop, calls=%fused_computation.2 | loop fusion | bytes 6291456 | tf_op jit(solution)/shard_map/cond/branch_1_fun/squeeze | solution.py:549
  29.1 4.1 %collective-permute-done.8 = bf16[256,512]{1,0:T(8,128)(2,1)S(1)} collective-permute-done((bf16[256,512]{1,0:T(8,128)(2,1)}, bf16[256,512]{1,0:T(8,128)(2,1)S(1)}, u32[]{:S(2)}, u32[]{:S(2)}) %collective-permute-start.8) | collective-permute-done | bytes 262176 | tf_op jit(solution)/shard_map/cond/branch_1_fun/ppermute | solution.py:39
  33.8 5.1 %collective-permute-done.5 = bf16[256,512]{1,0:T(8,128)(2,1)S(1)} collective-permute-done((bf16[256,512]{1,0:T(8,128)(2,1)}, bf16[256,512]{1,0:T(8,128)(2,1)S(1)}, u32[]{:S(2)}, u32[]{:S(2)}) %collective-permute-start.5) | collective-permute-done | bytes 262176 | tf_op jit(solution)/shard_map/cond/branch_1_fun/ppermute | solution.py:39
  38.8 3.9 %collective-permute-done.9 = bf16[256,512]{1,0:T(8,128)(2,1)S(1)} collective-permute-done((bf16[256,512]{1,0:T(8,128)(2,1)}, bf16[256,512]{1,0:T(8,128)(2,1)S(1)}, u32[]{:S(2)}, u32[]{:S(2)}) %collective-permute-start.9) | collective-permute-done | bytes 262176 | tf_op jit(solution)/shard_map/cond/branch_1_fun/ppermute | solution.py:39
  42.8 2.7 %bitcast_select_fusion.9 = (bf16[256,512]{1,0:T(8,128)(2,1)S(1)}, bf16[256,512]{1,0:T(8,128)(2,1)S(1)}, bf16[256,512]{1,0:T(8,128)(2,1)}, bf16[256,512]{1,0:T(8,...) fusion(bf16[256,512]{1,0:T(8,128)(2,1)S(1)} %collective-permute, ...), kind=kLoop, calls=%fused_computation.32 | loop fusion | flops 1048576 | bytes 4194313 | tf_op jit(solution)/shard_map/cond/branch_1_fun/jit(_where)/select_n | solution.py:45
  47.1 4.6 %branch_1_fun.6 = bf16[512,512]{1,0:T(8,128)(2,1)} custom-call(s32[2]{0:T(128)} %pad_add_fusion.meta, f32[4,16]{1,0:T(4,128)} %fusion.14.scales, bf16[512,512]{1,0:T(8,128)(2,1)} %pad_maximum_fusion.q_ref, bf16[512,512]{1,0:T(8,128)(2,1)} %pad_maximum_fusion.1.k_ref, bf16[512,512]{1,0:T(8,128)(2,1)} %pad_maximum_fusion.2.v_ref), custom_call_target="tpu_custom_call" | custom-call | flops 536870912 | bytes 2097152 | tf_op jit(solution)/shard_map/cond/branch_1_fun/pallas_call | solution.py:113
  52.3 1.8 pad_maximum_fusion.3.q_ref
  54.0 1.9 pad_maximum_fusion.5.v_ref
  56.0 1.9 pad_maximum_fusion.4.k_ref
  57.8 4.6 %branch_1_fun.7 = bf16[512,512]{1,0:T(8,128)(2,1)} custom-call(s32[2]{0:T(128)} %pad_add_fusion.1.meta, f32[4,16]{1,0:T(4,128)} %fusion.14.scales, bf16[512,512]{1,0:T(8,128)(2,1)} %pad_maximum_fusion.3.q_ref, bf16[512,512]{1,0:T(8,128)(2,1)} %pad_maximum_fusion.4.k_ref, bf16[512,512]{1,0:T(8,128)(2,1)} %pad_maximum_fusion.5.v_ref), custom_call_target="tpu_custom_call" | custom-call | flops 536870912 | bytes 2097152 | tf_op jit(solution)/shard_map/cond/branch_1_fun/pallas_call | solution.py:113
  67.1 8.5 %collective-permute-done.10 = bf16[512,512]{1,0:T(8,128)(2,1)S(1)} collective-permute-done((bf16[512,512]{1,0:T(8,128)(2,1)}, bf16[512,512]{1,0:T(8,128)(2,1)S(1)}, u32[]{:S(2)}, u32[]{:S(2)}) %collective-permute-start.10) | collective-permute-done | bytes 524320 | tf_op jit(solution)/shard_map/cond/branch_1_fun/ppermute | solution.py:39
  77.2 19.1 %collective-permute-done.1 = bf16[2048,1024]{1,0:T(8,128)(2,1)} collective-permute-done((bf16[2048,1024]{1,0:T(8,128)(2,1)}, bf16[2048,1024]{1,0:T(8,128)(2,1)}, u32[]{:S(2)}, u32[]{:S(2)}) %collective-permute-start.1) | collective-permute-done | bytes 4194336 | tf_op jit(solution)/shard_map/cond/branch_1_fun/ppermute | solution.py:29
  96.3 8.3 %fusion.tracker_ref = bf16[2048,1024]{1,0:T(8,128)(2,1)} fusion(bf16[2048,1024]{1,0:T(8,128)(2,1)} %collective-permute-done.1, bf16[1,2048,1024]{2,1,0:T(8,128)(2,1)} %get-tuple-element.93, bf16[512,512]{1,0:T(8,128)(2,1)S(1)} %get-tuple-element.133, bf16[512,512]{1,0:T(8,128)(2,1)S(1)} %get-tuple-element.131, bf16[512,512]{1,0:T(8,128)(2,1)S(1)} %get-tuple-element.132, ...), kind=kOutput, calls=%fused_computation.1 | convolution fusion | flops 2173173760 | bytes 19923456 | tf_op jit(solution)/shard_map/cond/branch_1_fun/dot_general | solution.py:33
  104.6 59.0 %collective-permute-done.13.peer_ref = bf16[1536,1024]{1,0:T(8,128)(2,1)S(1)} collective-permute-done((bf16[1536,1024]{1,0:T(8,128)(2,1)}, bf16[1536,1024]{1,0:T(8,128)(2,1)S(1)}, u32[]{:S(2)}, u32[]{:S(2)}) %collective-permute-start.13) | collective-permute-done | bytes 3145760 | tf_op jit(solution)/shard_map/cond/branch_1_fun/ppermute | solution.py:29
  163.6 5.9 %branch_1_fun.8.rest_0_ = bf16[2048,1024]{1,0:T(8,128)(2,1)} custom-call(bf16[2048,1024]{1,0:T(8,128)(2,1)S(1)} %bitcast.174, bf16[1536,1024]{1,0:T(8,128)(2,1)S(1)} %collective-permute-done.13.peer_ref, bf16[2048,1024]{1,0:T(8,128)(2,1)} %fusion.tracker_ref), custom_call_target="tpu_custom_call" | custom-call | flops 6291456 | bytes 12582912 | tf_op jit(solution)/shard_map/cond/branch_1_fun/pallas_call | solution.py:146
  169.5 15.7 %collective-permute-done.12.peer_ref = bf16[384,1024]{1,0:T(8,128)(2,1)S(1)} collective-permute-done((bf16[384,1024]{1,0:T(8,128)(2,1)S(1)}, bf16[384,1024]{1,0:T(8,128)(2,1)S(1)}, u32[]{:S(2)}, u32[]{:S(2)}) %collective-permute-start.12) | collective-permute-done | bytes 786464 | tf_op jit(solution)/shard_map/cond/branch_1_fun/ppermute | solution.py:29
  185.2 2.4 %branch_1_fun.9.rest_0_ = bf16[2048,1024]{1,0:T(8,128)(2,1)} custom-call(bf16[2048,1024]{1,0:T(8,128)(2,1)S(1)} %bitcast.175, bf16[384,1024]{1,0:T(8,128)(2,1)S(1)} %collective-permute-done.12.peer_ref, bf16[2048,1024]{1,0:T(8,128)(2,1)} %fusion.tracker_ref, bf16[2048,1024]{1,0:T(8,128)(2,1)} %branch_1_fun.8.rest_0_), custom_call_target="tpu_custom_call", output_to_operand_aliasing={{}: (3, {})} | custom-call | flops 1572864 | bytes 3145728 | tf_op jit(solution)/shard_map/cond/branch_1_fun/pallas_call | solution.py:146
  187.6 1.6 branch_1_fun.10.rest_0_
  189.3 1.6 branch_1_fun.11
  (45 shorter events, 24.3 us)
Async XLA Ops:
  1.5 94.8 %collective-permute-start.1 = (bf16[2048,1024]{1,0:T(8,128)(2,1)}, bf16[2048,1024]{1,0:T(8,128)(2,1)}, u32[]{:S(2)}, u32[]{:S(2)}) collective-permute-start(bf16[2048,1024]{1,0:T(8,128)(2,1)} %bitcast.190), channel_id=1, source_target_pairs={{0,4},{2,6},{4,0},{6,2},{8,12},{10,14},{12,8},{14,10},{16,20},{18,... | collective-permute-start | bytes 12582920 | tf_op jit(solution)/shard_map/cond/branch_1_fun/ppermute | solution.py:29
  4.5 17.6 %collective-permute-start.2 = (s32[2,16]{1,0:T(2,128)}, s32[2,16]{1,0:T(2,128)S(1)}, u32[]{:S(2)}, u32[]{:S(2)}) collective-permute-start(s32[2,16]{1,0:T(2,128)} %bitcast.196), channel_id=1, source_target_pairs={{0,1},{1,0},{2,3},{3,2},{4,5},{5,4},{6,7},{7,6},{8,9},{9,8},{10,11... | collective-permute-start | bytes 392 | tf_op jit(solution)/shard_map/cond/branch_1_fun/ppermute | solution.py:39
  7.1 17.1 %collective-permute-start.3 = (bf16[256,512]{1,0:T(8,128)(2,1)S(1)}, bf16[256,512]{1,0:T(8,128)(2,1)S(1)}, u32[]{:S(2)}, u32[]{:S(2)}) collective-permute-start(bf16[256,512]{1,0:T(8,128)(2,1)S(1)} %get-tuple-element.144), channel_id=1, source_target_pairs={{0,1},{1,0},{2,3},{3,2},{4,5},{5,4},{6,7},{7,6},{8,9},{9,8},{10,11... | collective-permute-start | bytes 786440 | tf_op jit(solution)/shard_map/cond/branch_1_fun/ppermute | solution.py:39
  7.7 17.1 %collective-permute-start.7 = (bf16[256,512]{1,0:T(8,128)(2,1)S(1)}, bf16[256,512]{1,0:T(8,128)(2,1)S(1)}, u32[]{:S(2)}, u32[]{:S(2)}) collective-permute-start(bf16[256,512]{1,0:T(8,128)(2,1)S(1)} %get-tuple-element.145), channel_id=1, source_target_pairs={{0,1},{1,0},{2,3},{3,2},{4,5},{5,4},{6,7},{7,6},{8,9},{9,8},{10,11... | collective-permute-start | bytes 786440 | tf_op jit(solution)/shard_map/cond/branch_1_fun/ppermute | solution.py:39
  11.0 12.6 %copy-start.15 = (s32[1,2,16]{2,1,0:T(2,128)S(1)}, s32[1,2,16]{2,1,0:T(2,128)}, u32[]{:S(2)}) copy-start(s32[1,2,16]{2,1,0:T(2,128)} %get-tuple-element.88) | copy-start | bytes 388 | tf_op jit(solution)/shard_map/cond
  11.0 15.3 %copy-start.3 = (bf16[1,256,2048]{2,1,0:T(8,128)(2,1)S(1)}, bf16[1,256,2048]{2,1,0:T(8,128)(2,1)}, u32[]{:S(2)}) copy-start(bf16[1,256,2048]{2,1,0:T(8,128)(2,1)} %get-tuple-element.89) | copy-start | bytes 3145732 | tf_op jit(solution)/shard_map/cond
  11.0 16.7 %collective-permute-start.4 = (bf16[256,512]{1,0:T(8,128)(2,1)S(1)}, bf16[256,512]{1,0:T(8,128)(2,1)}, u32[]{:S(2)}, u32[]{:S(2)}) collective-permute-start(bf16[256,512]{1,0:T(8,128)(2,1)S(1)} %get-tuple-element.140), channel_id=1, source_target_pairs={{0,1},{1,0},{2,3},{3,2},{4,5},{5,4},{6,7},{7,6},{8,9},{9,8},{10,11... | collective-permute-start | bytes 786440 | tf_op jit(solution)/shard_map/cond/branch_1_fun/ppermute | solution.py:39
  22.1 11.1 %collective-permute-start.8 = (bf16[256,512]{1,0:T(8,128)(2,1)}, bf16[256,512]{1,0:T(8,128)(2,1)S(1)}, u32[]{:S(2)}, u32[]{:S(2)}) collective-permute-start(bf16[256,512]{1,0:T(8,128)(2,1)} %get-tuple-element.141), channel_id=1, source_target_pairs={{0,1},{1,0},{2,3},{3,2},{4,5},{5,4},{6,7},{7,6},{8,9},{9,8},{10,11... | collective-permute-start | bytes 786440 | tf_op jit(solution)/shard_map/cond/branch_1_fun/ppermute | solution.py:39
  24.2 14.6 %collective-permute-start.5 = (bf16[256,512]{1,0:T(8,128)(2,1)}, bf16[256,512]{1,0:T(8,128)(2,1)S(1)}, u32[]{:S(2)}, u32[]{:S(2)}) collective-permute-start(bf16[256,512]{1,0:T(8,128)(2,1)} %get-tuple-element.136), channel_id=1, source_target_pairs={{0,1},{1,0},{2,3},{3,2},{4,5},{5,4},{6,7},{7,6},{8,9},{9,8},{10,11... | collective-permute-start | bytes 786440 | tf_op jit(solution)/shard_map/cond/branch_1_fun/ppermute | solution.py:39
  24.7 18.0 %collective-permute-start.9 = (bf16[256,512]{1,0:T(8,128)(2,1)}, bf16[256,512]{1,0:T(8,128)(2,1)S(1)}, u32[]{:S(2)}, u32[]{:S(2)}) collective-permute-start(bf16[256,512]{1,0:T(8,128)(2,1)} %get-tuple-element.137), channel_id=1, source_target_pairs={{0,1},{1,0},{2,3},{3,2},{4,5},{5,4},{6,7},{7,6},{8,9},{9,8},{10,11... | collective-permute-start | bytes 786440 | tf_op jit(solution)/shard_map/cond/branch_1_fun/ppermute | solution.py:39
  27.7 135.9 %collective-permute-start.13 = (bf16[1536,1024]{1,0:T(8,128)(2,1)}, bf16[1536,1024]{1,0:T(8,128)(2,1)S(1)}, u32[]{:S(2)}, u32[]{:S(2)}) collective-permute-start(bf16[1536,1024]{1,0:T(8,128)(2,1)} %slice_bitcast_fusion), channel_id=1, source_target_pairs={{0,4},{2,6},{4,0},{6,2},{8,12},{10,14},{12,8},{14,10},{16,20},{18,... | collective-permute-start | bytes 9437192 | tf_op jit(solution)/shard_map/cond/branch_1_fun/ppermute | solution.py:29
  33.2 154.4 %collective-permute-start.11 = (bf16[64,1024]{1,0:T(8,128)(2,1)}, bf16[64,1024]{1,0:T(8,128)(2,1)S(1)}, u32[]{:S(2)}, u32[]{:S(2)}) collective-permute-start(bf16[64,1024]{1,0:T(8,128)(2,1)} %get-tuple-element.116), channel_id=1, source_target_pairs={{0,4},{2,6},{4,0},{6,2},{8,12},{10,14},{12,8},{14,10},{16,20},{18,... | collective-permute-start | bytes 393224 | tf_op jit(solution)/shard_map/cond/branch_1_fun/ppermute | solution.py:29
  51.8 13.4 %collective-permute-start.6 = (bf16[512,512]{1,0:T(8,128)(2,1)}, bf16[512,512]{1,0:T(8,128)(2,1)}, u32[]{:S(2)}, u32[]{:S(2)}) collective-permute-start(bf16[512,512]{1,0:T(8,128)(2,1)} %branch_1_fun.6), channel_id=1, source_target_pairs={{0,1},{1,0},{2,3},{3,2},{4,5},{5,4},{6,7},{7,6},{8,9},{9,8},{10,11... | collective-permute-start | bytes 1572872 | tf_op jit(solution)/shard_map/cond/branch_1_fun/ppermute | solution.py:39
  54.0 11.1 %copy-start.12 = (bf16[64,1024]{1,0:T(8,128)(2,1)S(1)}, bf16[64,1024]{1,0:T(8,128)(2,1)}, u32[]{:S(2)}) copy-start(bf16[64,1024]{1,0:T(8,128)(2,1)} %get-tuple-element.117) | copy-start | bytes 393220 | tf_op jit(solution)/shard_map/cond
  62.4 33.9 %copy-start.6 = (bf16[1,2048,1024]{2,1,0:T(8,128)(2,1)S(1)}, bf16[1,2048,1024]{2,1,0:T(8,128)(2,1)}, u32[]{:S(2)}) copy-start(bf16[1,2048,1024]{2,1,0:T(8,128)(2,1)} %get-tuple-element.86) | copy-start | bytes 12582916 | tf_op jit(solution)/shard_map/cond
  62.4 33.9 %copy-start.9 = (bf16[1,512,1024]{2,1,0:T(8,128)(2,1)S(1)}, bf16[1,512,1024]{2,1,0:T(8,128)(2,1)}, u32[]{:S(2)}) copy-start(bf16[1,512,1024]{2,1,0:T(8,128)(2,1)} %get-tuple-element.92) | copy-start | bytes 3145732 | tf_op jit(solution)/shard_map/cond
  62.4 13.1 %collective-permute-start.10 = (bf16[512,512]{1,0:T(8,128)(2,1)}, bf16[512,512]{1,0:T(8,128)(2,1)S(1)}, u32[]{:S(2)}, u32[]{:S(2)}) collective-permute-start(bf16[512,512]{1,0:T(8,128)(2,1)} %branch_1_fun.7), channel_id=1, source_target_pairs={{0,1},{1,0},{2,3},{3,2},{4,5},{5,4},{6,7},{7,6},{8,9},{9,8},{10,11... | collective-permute-start | bytes 1572872 | tf_op jit(solution)/shard_map/cond/branch_1_fun/ppermute | solution.py:39
  65.2 124.1 %collective-permute-start = (bf16[64,1024]{1,0:T(8,128)(2,1)S(1)}, bf16[64,1024]{1,0:T(8,128)(2,1)S(1)}, u32[]{:S(2)}, u32[]{:S(2)}) collective-permute-start(bf16[64,1024]{1,0:T(8,128)(2,1)S(1)} %copy-done.12), channel_id=1, source_target_pairs={{0,4},{2,6},{4,0},{6,2},{8,12},{10,14},{12,8},{14,10},{16,20},{18,... | collective-permute-start | bytes 393224 | tf_op jit(solution)/shard_map/cond/branch_1_fun/ppermute | solution.py:29
  75.5 109.7 %collective-permute-start.12 = (bf16[384,1024]{1,0:T(8,128)(2,1)S(1)}, bf16[384,1024]{1,0:T(8,128)(2,1)S(1)}, u32[]{:S(2)}, u32[]{:S(2)}) collective-permute-start(bf16[384,1024]{1,0:T(8,128)(2,1)S(1)} %slice_bitcast_fusion.1), channel_id=1, source_target_pairs={{0,4},{2,6},{4,0},{6,2},{8,12},{10,14},{12,8},{14,10},{16,20},{18,... | collective-permute-start | bytes 2359304 | tf_op jit(solution)/shard_map/cond/branch_1_fun/ppermute | solution.py:29
  96.3 67.3 %copy-start = (bf16[1,2048,1024]{2,1,0:T(8,128)(2,1)S(1)}, bf16[1,2048,1024]{2,1,0:T(8,128)(2,1)}, u32[]{:S(2)}) copy-start(bf16[1,2048,1024]{2,1,0:T(8,128)(2,1)} %get-tuple-element.85) | copy-start | bytes 12582916 | tf_op jit(solution)/shard_map/cond
